TPU v7x, 32 devices: a whole 2x2x4 slice. The times are simulated.
32 devices in a mesh: groups: 2 (over y), expert: 4 (over z), dp: 2 (over x), inner: 2 (over core).
Axes of the slice: x: 2, y: 2, z: 4, core: 2. Of those that a mesh axis runs over, the one named last changes fastest.
Arguments:
- tokens: bfloat16 [2048, 1536], P(('groups', 'expert', 'dp'), 'inner'), parts along dimension 0, may hold values from -6 to 6
- out_grad: bfloat16 [2048, 1536], P(('groups', 'expert', 'dp'), 'inner'), parts along dimension 0, may hold values from -6 to 6
- expert_ids: int32 [2048, 8], P(('groups', 'expert', 'dp')), parts along dimension 0, may hold values from 0 to 63, all different within a row; in each aligned block of 128 rows (0 to 127, 128 to 255, ...) at most 17 rows name the same one
- gate_probs: float32 [2048, 8], P(('groups', 'expert', 'dp')), parts along dimension 0, may hold values from 0.05 to 0.5
- gate_weight: bfloat16 [64, 1536, 384], P('expert', 'inner', 'dp'), may hold values from -0.15625 to 0.15625
- up_weight: bfloat16 [64, 1536, 384], P('expert', 'inner', 'dp'), may hold values from -0.15625 to 0.15625
- down_weight: bfloat16 [64, 384, 1536], P('expert', 'dp', 'inner'), may hold values from -0.3125 to 0.3125
Outputs:
- token_grad: bfloat16 [2048, 1536], P(('groups', 'expert', 'dp'), 'inner'), parts along dimension 0
- prob_grad: float32 [2048, 8], P(('groups', 'expert', 'dp')), parts along dimension 0
- gate_weight_grad: bfloat16 [128, 1536, 384], P(('groups', 'expert'), 'inner', 'dp'), parts along dimension 0
- up_weight_grad: bfloat16 [128, 1536, 384], P(('groups', 'expert'), 'inner', 'dp'), parts along dimension 0
- down_weight_grad: bfloat16 [128, 384, 1536], P(('groups', 'expert'), 'dp', 'inner'), parts along dimension 0
There are 2 independent parts, one for each index of `groups`. A program takes and returns all parts, laid end to end along the dimension named above; an argument that names none is the same for every part. Nothing has to cross between parts.
Inputs may be any that keep to these rules, and one draw needn't show every extreme that they name: `expert_ids`: within the rows of one block of 128 tokens no expert is chosen more than 17 times, and some expert is chosen exactly 17 times in some block; a token's 8 experts differ.
All inputs are finite; a program needn't handle non-finite values.
Results may differ from a plain program's by a relative error of at most 0.015.
Values may be sent and summed in bfloat16 or wider, within the bound.
A program may use at most 192 MiB of HBM per device.

v0:
```python
import jax
import jax.numpy as jnp
from jax import lax
from jax.sharding import PartitionSpec as P


def on_device(tokens, out_grad, expert_ids, gate_probs, gate_weight, up_weight, down_weight):
    tok_rows, width_half = tokens.shape
    top_count = expert_ids.shape[1]
    per_dev = gate_weight.shape[0]
    owners = lax.axis_size("expert")
    experts = per_dev * owners
    capacity = tok_rows * top_count // experts + 1
    row_count = owners * capacity
    total_slots = experts * capacity
    pair_count = tok_rows * top_count
    chosen = expert_ids.reshape(-1)
    matches = (chosen[:, None] == jnp.arange(experts, dtype=jnp.int32)[None, :]).astype(jnp.int32)
    before = jnp.cumsum(matches, axis=0) - matches
    slot_index = jnp.sum(before * matches, axis=1)
    target = chosen % per_dev * row_count + chosen // per_dev * capacity + slot_index
    source_tok = (
        jnp.zeros((total_slots,), jnp.int32)
        .at[target]
        .set(jnp.arange(pair_count, dtype=jnp.int32) // top_count)
    )
    filled = jnp.zeros((total_slots,), jnp.bfloat16).at[target].set(1)
    slot_probs = (
        jnp.zeros((total_slots,), jnp.float32)
        .at[target]
        .set(gate_probs.reshape(-1))
        .astype(jnp.bfloat16)
    )
    sent_rows = (tokens[source_tok] * filled[:, None]).reshape(
        per_dev, owners, capacity, width_half
    )
    sent_grads = (out_grad[source_tok] * filled[:, None]).reshape(
        per_dev, owners, capacity, width_half
    )
    sent_probs = slot_probs.reshape(per_dev, owners, capacity)
    arrived_rows, arrived_grads, arrived_probs = (
        lax.all_to_all(sent_rows, "expert", split_axis=1, concat_axis=1, tiled=True),
        lax.all_to_all(sent_grads, "expert", split_axis=1, concat_axis=1, tiled=True),
        lax.all_to_all(sent_probs, "expert", split_axis=1, concat_axis=1, tiled=True),
    )
    full_gate, full_up, full_down = (
        lax.all_gather(gate_weight, "dp", axis=2, tiled=True),
        lax.all_gather(up_weight, "dp", axis=2, tiled=True),
        lax.all_gather(down_weight, "dp", axis=1, tiled=True),
    )
    expert_rows = arrived_rows.reshape(per_dev, row_count, width_half)
    gate_part = jnp.einsum(
        "jrd,jdf->jrf", expert_rows, full_gate, preferred_element_type=jnp.float32
    )
    up_part = jnp.einsum("jrd,jdf->jrf", expert_rows, full_up, preferred_element_type=jnp.float32)
    gate_sum, up_sum = (
        lax.psum(gate_part.astype(jnp.bfloat16), "inner").astype(jnp.float32),
        lax.psum(up_part.astype(jnp.bfloat16), "inner").astype(jnp.float32),
    )
    sigmoid_gate = jax.nn.sigmoid(gate_sum)
    activated = gate_sum * sigmoid_gate
    hidden = (activated * up_sum).astype(jnp.bfloat16)
    expert_grads = arrived_grads.reshape(per_dev, row_count, width_half)
    prob_col = arrived_probs.reshape(per_dev, row_count, 1).astype(jnp.float32)
    slope_part = jnp.einsum(
        "jrd,jfd->jrf", expert_grads, full_down, preferred_element_type=jnp.float32
    )
    slope_sum = lax.psum(slope_part.astype(jnp.bfloat16), "inner").astype(jnp.float32)
    scores = jnp.sum(hidden.astype(jnp.float32) * slope_sum, axis=-1)
    hidden_grad = prob_col * slope_sum
    gate_back = (
        hidden_grad * up_sum * sigmoid_gate * (1.0 + gate_sum * (1.0 - sigmoid_gate))
    ).astype(jnp.bfloat16)
    up_back = (hidden_grad * activated).astype(jnp.bfloat16)
    row_grads = jnp.einsum("jrf,jdf->jrd", gate_back, full_gate, preferred_element_type=jnp.float32)
    row_grads = (
        row_grads + jnp.einsum("jrf,jdf->jrd", up_back, full_up, preferred_element_type=jnp.float32)
    ).astype(jnp.bfloat16)
    returned_rows, returned_scores = (
        lax.all_to_all(
            row_grads.reshape(per_dev, owners, capacity, width_half),
            "expert",
            split_axis=1,
            concat_axis=1,
            tiled=True,
        ),
        lax.all_to_all(
            scores.astype(jnp.bfloat16).reshape(per_dev, owners, capacity),
            "expert",
            split_axis=1,
            concat_axis=1,
            tiled=True,
        ),
    )
    pair_rows = returned_rows.reshape(total_slots, width_half)[target]
    token_grad = jnp.sum(
        pair_rows.reshape(tok_rows, top_count, width_half).astype(jnp.float32), axis=1
    ).astype(jnp.bfloat16)
    prob_grad = returned_scores.reshape(-1)[target].astype(jnp.float32).reshape(tok_rows, top_count)
    grad_gate = jnp.einsum(
        "jrd,jrf->jdf", expert_rows, gate_back, preferred_element_type=jnp.float32
    )
    grad_up = jnp.einsum("jrd,jrf->jdf", expert_rows, up_back, preferred_element_type=jnp.float32)
    down_rows = (prob_col * expert_grads).astype(jnp.bfloat16)
    grad_down = jnp.einsum("jrf,jrd->jfd", hidden, down_rows, preferred_element_type=jnp.float32)
    summed_gate, summed_up, summed_down = (
        lax.psum_scatter(
            grad_gate.astype(jnp.bfloat16), "dp", scatter_dimension=2, tiled=True
        ).astype(jnp.float32),
        lax.psum_scatter(
            grad_up.astype(jnp.bfloat16), "dp", scatter_dimension=2, tiled=True
        ).astype(jnp.float32),
        lax.psum_scatter(
            grad_down.astype(jnp.bfloat16), "dp", scatter_dimension=1, tiled=True
        ).astype(jnp.float32),
    )
    return (
        token_grad,
        prob_grad,
        summed_gate.astype(jnp.bfloat16),
        summed_up.astype(jnp.bfloat16),
        summed_down.astype(jnp.bfloat16),
    )


def solution(mesh):
    placed = (
        P(("groups", "expert", "dp"), "inner"),
        P(("groups", "expert", "dp"), "inner"),
        P(("groups", "expert", "dp"), None),
        P(("groups", "expert", "dp"), None),
        P("expert", "inner", "dp"),
        P("expert", "inner", "dp"),
        P("expert", "dp", "inner"),
    )
    return jax.shard_map(
        on_device,
        mesh=mesh,
        in_specs=placed,
        out_specs=(
            P(("groups", "expert", "dp"), "inner"),
            P(("groups", "expert", "dp"), None),
            P(("groups", "expert"), "inner", "dp"),
            P(("groups", "expert"), "inner", "dp"),
            P(("groups", "expert"), "dp", "inner"),
        ),
        check_vma=False,
    )
```

profile of v0, /device:TPU:0, one launch (start us, length us, event | category | flops | bytes accessed | tf_op | source)
XLA Modules:
  0.0 753.5 jit_solution(1835674188766818200)
XLA Ops:
  7.2 0.7 all-gather.6.cloned.1.call-update
  8.0 0.7 all-gather.8.cloned.1.call-update
  8.7 0.7 all-gather.4.cloned.1.call-update
  9.8 18.0 %reduce-window.6 = s32[64,8,128]{2,1,0:T(8,128)S(1)} reduce-window(s32[64,8,128]{2,1,0:T(8,128)S(1)} %fusion.24, s32[]{:T(128)} %constant.51.clone.1), window={size=1x1x128 pad=0_0x0_0x127_0}, to_apply=%region_0.0 | reduce-window | flops 8323072 | bytes 524292 | tf_op jit(solution)/shard_map/reduce-window
  28.5 4.3 scatter_custom_fusion.1
  32.9 4.8 gather_fusion.1
  37.7 2.5 gather.19
  40.2 7.6 %scatter_custom_fusion.2 = bf16[1088]{0:T(1024)(128)(2,1)S(1)} fusion(s32[1024]{0:T(1024)S(1)} %bitcast.54, bf16[1024]{0:T(1024)(128)(2,1)S(1)} %broadcast.149, bf16[]{:T(256)} %constant.63.clone.1), kind=kCustom, calls=%fused_computation.74 | custom fusion | bytes 2178 | tf_op jit(solution)/shard_map/scatter | solution.py:27
  48.0 4.8 gather_fusion
  52.8 3.6 gather.17
  56.4 3.4 broadcast_multiply_fusion
  59.8 2.1 copy.58
  61.9 6.3 all-to-all-start.2
  68.3 3.8 copy.56
  72.1 35.3 %all-to-all-done.2 = bf16[16,4,17,768]{3,0,2,1:T(8,128)(2,1)S(1)} async-done(((bf16[16,4,17,768]{3,0,2,1:T(8,128)(2,1)}), bf16[16,4,17,768]{3,0,2,1:T(8,128)(2,1)S(1)}, u32[]{:S(2)}, u32[]{:S(2)}) %all-to-all-start.2) | async-done | bytes 1671200 | tf_op jit(solution)/shard_map/all_to_all | solution.py:42
  107.3 3.6 all-to-all-start.1
  111.4 18.8 %all-gather.6.cloned.1.call-done = bf16[16,768,384]{1,2,0:T(8,128)(2,1)} async-done(((bf16[16,768,192]{1,2,0:T(8,128)(2,1)}), bf16[16,768,384]{1,2,0:T(8,128)(2,1)}) %all-gather.6.cloned.1.call-update) | async-done | bytes 9437200 | tf_op jit(solution)/shard_map/all_gather | solution.py:48
  130.2 7.4 convolution_convert_fusion.4
  137.7 112.2 %all-gather.8.cloned.1.call-done = bf16[16,768,384]{1,2,0:T(8,128)(2,1)} async-done(((bf16[16,768,192]{1,2,0:T(8,128)(2,1)}), bf16[16,768,384]{1,2,0:T(8,128)(2,1)}) %all-gather.8.cloned.1.call-update) | async-done | bytes 9437200 | tf_op jit(solution)/shard_map/all_gather | solution.py:47
  249.8 7.5 convolution_convert_fusion.3
  257.3 112.0 %all-gather.4.cloned.1.call-done = bf16[16,384,768]{2,1,0:T(8,128)(2,1)} async-done(((bf16[16,192,768]{2,1,0:T(8,128)(2,1)}), bf16[16,384,768]{2,1,0:T(8,128)(2,1)}) %all-gather.4.cloned.1.call-update) | async-done | bytes 9437200 | tf_op jit(solution)/shard_map/all_gather | solution.py:49
  369.3 7.5 fusion.14
  377.7 4.3 scatter_custom_fusion
  382.3 10.0 %all_to_all.25 = bf16[4,2,136]{2,1,0:T(2,128)(2,1)S(1)} all-to-all(bf16[4,2,136]{2,1,0:T(2,128)(2,1)S(1)} %reshape.281), channel_id=1, replica_groups=mesh['groups'=2,'expert'=4,'dp'=2,'inner'=2] {'expert'}, dimensions={0} | all-to-all | bytes 4352 | tf_op jit(solution)/shard_map/all_to_all | solution.py:44
  392.5 7.0 all-reduce.3.cloned.1.call-done
  399.5 8.3 %convolution_convert_fusion.2 = bf16[16,768,384]{1,2,0:T(8,128)(2,1)} fusion(bf16[16,68,768]{2,0,1:T(8,128)(2,1)S(1)} %bitcast.41, bf16[16,68,384]{2,1,0:T(8,128)(2,1)} %get-tuple-element.21, bf16[16,68,384]{2,1,0:T(8,128)(2,1)} %get-tuple-element.20, bf16[16,68,384]{2,1,0:T(8,128)(2,1)} %get-tuple-element.22, f32[16,68]{1,0:T(8,128)S(1)} %reshape.215), kind=kOutput, calls=%fused_computation.9 | convolution fusion | flops 652296192 | bytes 13619456 | tf_op jit(solution)/shard_map/jrd,jrf->jdf/dot_general | solution.py:100
  408.0 8.2 %convolution_convert_fusion.1 = bf16[16,768,384]{1,2,0:T(8,128)(2,1)} fusion(bf16[16,68,768]{2,0,1:T(8,128)(2,1)S(1)} %bitcast.42, bf16[16,68,384]{2,1,0:T(8,128)(2,1)} %get-tuple-element.20, f32[16,68]{1,0:T(8,128)S(1)} %reshape.215, bf16[16,68,384]{2,1,0:T(8,128)(2,1)} %get-tuple-element.22), kind=kOutput, calls=%fused_computation.8 | convolution fusion | flops 650207232 | bytes 12783872 | tf_op jit(solution)/shard_map/jrd,jrf->jdf/dot_general | solution.py:103
  416.8 0.7 copy-done.4
  417.4 7.6 %convolution_convert_fusion = bf16[16,384,768]{2,1,0:T(8,128)(2,1)} fusion(bf16[16,68,768]{2,0,1:T(8,128)(2,1)S(1)} %multiply_convert_fusion, bf16[16,68,384]{2,1,0:T(8,128)(2,1)} %get-tuple-element.21, bf16[16,68,384]{2,1,0:T(8,128)(2,1)S(1)} %copy-done.4), kind=kOutput, calls=%fused_computation.7 | convolution fusion | flops 649789440 | bytes 12779520 | tf_op jit(solution)/shard_map/jrf,jrd->jfd/dot_general | solution.py:105
  425.0 1.2 copy-done.3
  426.2 2.1 fusion.2
  428.3 0.7 reshape.283
  429.0 4.8 all-to-all-start.4
  433.9 6.1 fusion.41
  440.0 0.6 slice-done.2
  440.6 2.0 add_convert_fusion
  442.6 1.5 copy.61
  444.1 5.3 all-to-all-start.3
  449.7 6.8 gather_fusion.3
  456.6 0.7 copy.69
  457.2 31.1 %all-to-all-done.3 = bf16[16,4,17,768]{3,0,2,1:T(8,128)(2,1)S(1)} async-done(((bf16[16,4,17,768]{3,0,2,1:T(8,128)(2,1)}), bf16[16,4,17,768]{3,0,2,1:T(8,128)(2,1)S(1)}, u32[]{:S(2)}, u32[]{:S(2)}) %all-to-all-start.3) | async-done | bytes 1671200 | tf_op jit(solution)/shard_map/all_to_all | solution.py:80
  488.3 2.1 copy.62
  490.4 2.7 reshape.212
  493.1 4.0 gather_fusion.2
  497.1 1.7 bitcast_reduce_fusion
  498.8 20.8 %reduce-scatter.4.cloned.1.call-done = bf16[16,768,192]{1,2,0:T(8,128)(2,1)} async-done(((bf16[16,768,384]{1,2,0:T(8,128)(2,1)}), bf16[16,768,192]{1,2,0:T(8,128)(2,1)}) %reduce-scatter.4.cloned.1.call-update) | async-done | bytes 4718608 | tf_op jit(solution)/shard_map/reduce_scatter | solution.py:107
  519.6 113.3 %reduce-scatter.6.cloned.1.call-done = bf16[16,768,192]{1,2,0:T(8,128)(2,1)} async-done(((bf16[16,768,384]{1,2,0:T(8,128)(2,1)}), bf16[16,768,192]{1,2,0:T(8,128)(2,1)}) %reduce-scatter.6.cloned.1.call-update) | async-done | bytes 4718608 | tf_op jit(solution)/shard_map/reduce_scatter | solution.py:110
  633.0 113.5 %reduce-scatter.8.cloned.1.call-done = bf16[16,192,768]{2,1,0:T(8,128)(2,1)} async-done(((bf16[16,384,768]{2,1,0:T(8,128)(2,1)}), bf16[16,192,768]{2,1,0:T(8,128)(2,1)}) %reduce-scatter.8.cloned.1.call-update) | async-done | bytes 4718608 | tf_op jit(solution)/shard_map/reduce_scatter | solution.py:113
  (67 shorter events, 4.3 us)
Async XLA Ops:
  7.2 25.7 %copy-start = (bf16[128,768]{1,0:T(8,128)(2,1)S(1)}, bf16[128,768]{1,0:T(8,128)(2,1)}, u32[]{:S(2)}) copy-start(bf16[128,768]{1,0:T(8,128)(2,1)} %param.7) | copy-start | bytes 589828
  7.2 123.1 %all-gather.6.cloned.1.call-start = ((), (), s32[]{:S(2)}) async-start(), calls=%async_computation.9 | async-start | bytes 14155776 | tf_op jit(solution)/shard_map/all_gather | solution.py:48
  7.9 241.9 %all-gather.8.cloned.1.call-start = ((), (), s32[]{:S(2)}) async-start(), calls=%async_computation.10 | async-start | bytes 14155776 | tf_op jit(solution)/shard_map/all_gather | solution.py:47
  8.7 0.7 copy-start.5
  8.7 360.6 %all-gather.4.cloned.1.call-start = ((), (), s32[]{:S(2)}) async-start(), calls=%async_computation.8 | async-start | bytes 14155776 | tf_op jit(solution)/shard_map/all_gather | solution.py:49
  37.7 10.3 %copy-start.2 = (bf16[128,768]{1,0:T(8,128)(2,1)S(1)}, bf16[128,768]{1,0:T(8,128)(2,1)}, u32[]{:S(2)}) copy-start(bf16[128,768]{1,0:T(8,128)(2,1)} %param.8) | copy-start | bytes 589828
  61.9 45.4 %all-to-all-start.2 = ((bf16[16,4,17,768]{3,0,2,1:T(8,128)(2,1)}), bf16[16,4,17,768]{3,0,2,1:T(8,128)(2,1)S(1)}, u32[]{:S(2)}, u32[]{:S(2)}) async-start(bf16[16,4,17,768]{3,0,2,1:T(8,128)(2,1)} %copy.58), calls=%async_computation.2 | async-start | bytes 3342336 | tf_op jit(solution)/shard_map/all_to_all | solution.py:42
  107.3 150.0 %all-to-all-start.1 = ((bf16[16,4,17,768]{3,0,2,1:T(8,128)(2,1)}), bf16[16,4,17,768]{3,0,2,1:T(8,128)(2,1)S(1)}, u32[]{:S(2)}, u32[]{:S(2)}) async-start(bf16[16,4,17,768]{3,0,2,1:T(8,128)(2,1)} %copy.56), calls=%async_computation.1 | async-start | bytes 3342336 | tf_op jit(solution)/shard_map/all_to_all | solution.py:43
  110.9 288.5 %all-reduce.3.cloned.1.call-start = ((), (), s32[]{:S(2)}) async-start(), calls=%async_computation.14 | async-start | bytes 5308416 | tf_op jit(solution)/shard_map/psum | solution.py:68
  376.8 0.7 copy-start.6
  376.8 142.8 %reduce-scatter.4.cloned.1.call-start = ((), (), s32[]{:S(2)}) async-start(), calls=%async_computation.11 | async-start | bytes 14155776 | tf_op jit(solution)/shard_map/reduce_scatter | solution.py:107
  407.8 225.2 %reduce-scatter.6.cloned.1.call-start = ((), (), s32[]{:S(2)}) async-start(), calls=%async_computation.12 | async-start | bytes 14155776 | tf_op jit(solution)/shard_map/reduce_scatter | solution.py:110
  416.2 1.2 copy-start.4
  416.2 330.2 %reduce-scatter.8.cloned.1.call-start = ((), (), s32[]{:S(2)}) async-start(), calls=%async_computation.13 | async-start | bytes 14155776 | tf_op jit(solution)/shard_map/reduce_scatter | solution.py:113
  425.0 1.2 copy-start.3
  426.2 13.8 %slice-start = ((s8[9437184]{0:T(1024)(128)(4,1)}), s8[1048576]{0:T(1024)(128)(4,1)S(1)}, s32[]{:S(2)}) async-start(s8[9437184]{0:T(1024)(128)(4,1)} %bitcast.44), calls=%async_computation.15 | async-start | bytes 2097152
  429.0 15.0 %all-to-all-start.4 = ((bf16[4,2,136]{2,1,0:T(2,128)(2,1)}), bf16[4,2,136]{2,1,0:T(2,128)(2,1)S(1)}, u32[]{:S(2)}, u32[]{:S(2)}) async-start(bf16[4,2,136]{2,1,0:T(2,128)(2,1)} %reshape.283), calls=%async_computation.4 | async-start | bytes 8192 | tf_op jit(solution)/shard_map/all_to_all | solution.py:87
  433.9 6.1 slice-start.1
  433.9 6.7 slice-start.2
  444.1 44.2 %all-to-all-start.3 = ((bf16[16,4,17,768]{3,0,2,1:T(8,128)(2,1)}), bf16[16,4,17,768]{3,0,2,1:T(8,128)(2,1)S(1)}, u32[]{:S(2)}, u32[]{:S(2)}) async-start(bf16[16,4,17,768]{3,0,2,1:T(8,128)(2,1)} %bitcast.6), calls=%async_computation.3 | async-start | bytes 3342336 | tf_op jit(solution)/shard_map/all_to_all | solution.py:80
  493.1 253.4 %copy-start.1 = (bf16[128,768]{1,0:T(8,128)(2,1)S(1)}, bf16[128,768]{1,0:T(8,128)(2,1)}, u32[]{:S(2)}) copy-start(bf16[128,768]{1,0:T(8,128)(2,1)} %param.7) | copy-start | bytes 589828
Sparse Core Ops, SparseCore 0:
  9.6 120.6 all-gather.5
  131.8 117.9 all-gather.7
  251.4 117.8 all-gather.3
  376.9 22.4 all-reduce.2
  407.9 111.6 reduce-scatter.3
  522.4 110.5 reduce-scatter.5
  635.9 110.5 reduce-scatter.7
where the time goes:
time: 762 us; the launch traced here: 754 us
  waiting for transfers between devices  566 us (74%)
  local copies, waits for them, and re-layouts  61.4 us (8%)
  matrix products  54.5 us (7%)
  other arithmetic  25.9 us (3%)
  starting transfers between devices  20.9 us (3%)
  between operations  14.7 us (2%)
  blocking collectives  10 us (1%)
    reduce_scatter x1, waiting for transfers between devices, on_device(): lax.psum_scatter(grad_down.astype(jnp.bfloat16), 'dp', scatter_dimension=...  113 us
    reduce_scatter x1, waiting for transfers between devices, on_device(): lax.psum_scatter(grad_up.astype(jnp.bfloat16), 'dp', scatter_dimension=2,...  113 us
    all_gather x1, waiting for transfers between devices, on_device(): lax.all_gather(gate_weight, 'dp', axis=2, tiled=True)  112 us
    all_gather x1, waiting for transfers between devices, on_device(): lax.all_gather(down_weight, 'dp', axis=1, tiled=True)  112 us
    all_to_all x1, waiting for transfers between devices, on_device(): lax.all_to_all(sent_rows, 'expert', split_axis=1, concat_axis=1, tiled=True)  35.3 us
    all_to_all x1, waiting for transfers between devices, on_device(): lax.all_to_all(row_grads.reshape(per_dev, owners, capacity, width_half),...  31.1 us
    reduce_scatter x1, waiting for transfers between devices, on_device(): lax.psum_scatter(grad_gate.astype(jnp.bfloat16), 'dp', scatter_dimension=...  20.8 us
    all_gather x1, waiting for transfers between devices, on_device(): lax.all_gather(up_weight, 'dp', axis=2, tiled=True)  18.8 us
  transfers between devices with their start and end apart: 11, of which 9 were waited for; matrix products, arithmetic and copies ran while one was open for 16% of the time, Pallas kernels for 0%

commit v1 on v0

--- a/solution.py
+++ b/solution.py
@@ -2,6 +2,28 @@
 import jax.numpy as jnp
 from jax import lax
 from jax.sharding import PartitionSpec as P
+
+
+def find_copies(xx, array_axis, values):
+    all_rows = xx.shape
+    return jnp.moveaxis(
+        xx.reshape(
+            *all_rows[:array_axis],
+            values,
+            all_rows[array_axis] // values,
+            *all_rows[array_axis + 1 :]
+        ),
+        array_axis,
+        0,
+    )
+
+
+def cover_copies(my_tile, where_dim):
+    my_tile = jnp.moveaxis(my_tile, 0, where_dim)
+    newest = my_tile.shape
+    return my_tile.reshape(
+        *newest[:where_dim], newest[where_dim] * newest[where_dim + 1], *newest[where_dim + 2 :]
+    )
 
 
 def on_device(tokens, out_grad, expert_ids, gate_probs, gate_weight, up_weight, down_weight):
@@ -76,14 +98,23 @@
     row_grads = (
         row_grads + jnp.einsum("jrf,jdf->jrd", up_back, full_up, preferred_element_type=jnp.float32)
     ).astype(jnp.bfloat16)
+
+    def advance_waves(mine, mesh_name, z, u):
+        v_next, all_values = (lax.axis_size(mesh_name), lax.axis_index(mesh_name))
+        local_part = find_copies(mine, z, v_next)
+        pile = [local_part[all_values]]
+        b = 1
+        while b < v_next:
+            reply = local_part[(all_values + b) % v_next]
+            pile.append(
+                lax.ppermute(reply, mesh_name, [(k0, (k0 + b) % v_next) for k0 in range(v_next)])
+            )
+            b += 1
+        local_part = jnp.stack(pile)[(all_values - jnp.arange(v_next)) % v_next]
+        return cover_copies(local_part, u)
+
     returned_rows, returned_scores = (
-        lax.all_to_all(
-            row_grads.reshape(per_dev, owners, capacity, width_half),
-            "expert",
-            split_axis=1,
-            concat_axis=1,
-            tiled=True,
-        ),
+        advance_waves(row_grads.reshape(per_dev, owners, capacity, width_half), "expert", 1, 1),
         lax.all_to_all(
             scores.astype(jnp.bfloat16).reshape(per_dev, owners, capacity),
             "expert",

time: 762 us -> 762 us (level)
    all_to_all x1 -> x0, waiting for transfers between devices: 31.1 us -> none  [on_device(): lax.all_to_all(row_grads.reshape(per_dev, owners, capacity, width_half),...]
    all_to_all x1, waiting for transfers between devices: 0.01 us -> 29.7 us  [on_device(): lax.all_to_all(scores.astype(jnp.bfloat16).reshape(per_dev, owners, capac...]
    another operation x3 -> x4, other arithmetic: 18.2 us -> 19.5 us
  transfers between devices with their start and end apart: 11 -> 13, of which waited for: 9 -> 9; matrix products, arithmetic and copies ran while one was open for 16% -> 16% of each run, Pallas kernels for 0% -> 0%
where the time goes in v1:
time: 762 us; the launch traced here: 753 us
  waiting for transfers between devices  565 us (74%)
  local copies, waits for them, and re-layouts  63.1 us (8%)
  matrix products  54.4 us (7%)
  other arithmetic  26 us (3%)
  starting transfers between devices  19.7 us (3%)
  between operations  14.7 us (2%)
  blocking collectives  10 us (1%)
    reduce_scatter x1, waiting for transfers between devices, on_device(): lax.psum_scatter(grad_down.astype(jnp.bfloat16), 'dp', scatter_dimension=...  113 us
    reduce_scatter x1, waiting for transfers between devices, on_device(): lax.psum_scatter(grad_up.astype(jnp.bfloat16), 'dp', scatter_dimension=2,...  113 us
    all_gather x1, waiting for transfers between devices, on_device(): lax.all_gather(gate_weight, 'dp', axis=2, tiled=True)  112 us
    all_gather x1, waiting for transfers between devices, on_device(): lax.all_gather(down_weight, 'dp', axis=1, tiled=True)  112 us
    all_to_all x1, waiting for transfers between devices, on_device(): lax.all_to_all(sent_rows, 'expert', split_axis=1, concat_axis=1, tiled=True)  35.3 us
    all_to_all x1, waiting for transfers between devices, on_device(): lax.all_to_all(scores.astype(jnp.bfloat16).reshape(per_dev, owners, capac...  29.7 us
    reduce_scatter x1, waiting for transfers between devices, on_device(): lax.psum_scatter(grad_gate.astype(jnp.bfloat16), 'dp', scatter_dimension=...  21.6 us
    all_gather x1, waiting for transfers between devices, on_device(): lax.all_gather(up_weight, 'dp', axis=2, tiled=True)  18.8 us
  transfers between devices with their start and end apart: 13, of which 9 were waited for; matrix products, arithmetic and copies ran while one was open for 16% of the time, Pallas kernels for 0%

profile of v1, /device:TPU:0, one launch (start us, length us, event | category | flops | bytes accessed | tf_op | source)
XLA Modules:
  0.0 753.4 jit_solution(9461595209076878775)
XLA Ops:
  8.0 0.7 all-gather.8.cloned.1.call-update
  8.7 0.7 all-gather.4.cloned.1.call-update
  9.8 18.0 %reduce-window.6 = s32[64,8,128]{2,1,0:T(8,128)S(1)} reduce-window(s32[64,8,128]{2,1,0:T(8,128)S(1)} %fusion.24, s32[]{:T(128)} %constant.85.clone.1), window={size=1x1x128 pad=0_0x0_0x127_0}, to_apply=%region_0.0 | reduce-window | flops 8323072 | bytes 524292 | tf_op jit(solution)/shard_map/reduce-window
  28.5 4.3 scatter_custom_fusion.1
  32.9 4.8 gather_fusion.1
  37.7 2.5 gather.22
  40.2 7.6 %scatter_custom_fusion.2 = bf16[1088]{0:T(1024)(128)(2,1)S(1)} fusion(s32[1024]{0:T(1024)S(1)} %bitcast.78, bf16[1024]{0:T(1024)(128)(2,1)S(1)} %broadcast.222, bf16[]{:T(256)} %constant.97.clone.1), kind=kCustom, calls=%fused_computation.84 | custom fusion | bytes 2178 | tf_op jit(solution)/shard_map/scatter | solution.py:49
  48.0 4.8 gather_fusion
  52.8 3.6 gather.20
  56.4 3.4 broadcast_multiply_fusion
  59.8 2.1 copy.58
  61.9 6.3 all-to-all-start.2
  68.3 3.8 copy.56
  72.1 35.3 %all-to-all-done.2 = bf16[16,4,17,768]{3,0,2,1:T(8,128)(2,1)S(1)} async-done(((bf16[16,4,17,768]{3,0,2,1:T(8,128)(2,1)}), bf16[16,4,17,768]{3,0,2,1:T(8,128)(2,1)S(1)}, u32[]{:S(2)}, u32[]{:S(2)}) %all-to-all-start.2) | async-done | bytes 1671200 | tf_op jit(solution)/shard_map/all_to_all | solution.py:64
  107.3 3.6 all-to-all-start.1
  111.4 18.8 %all-gather.6.cloned.1.call-done = bf16[16,768,384]{1,2,0:T(8,128)(2,1)} async-done(((bf16[16,768,192]{1,2,0:T(8,128)(2,1)}), bf16[16,768,384]{1,2,0:T(8,128)(2,1)}) %all-gather.6.cloned.1.call-update) | async-done | bytes 9437200 | tf_op jit(solution)/shard_map/all_gather | solution.py:70
  130.2 7.4 convolution_convert_fusion.4
  137.7 112.2 %all-gather.8.cloned.1.call-done = bf16[16,768,384]{1,2,0:T(8,128)(2,1)} async-done(((bf16[16,768,192]{1,2,0:T(8,128)(2,1)}), bf16[16,768,384]{1,2,0:T(8,128)(2,1)}) %all-gather.8.cloned.1.call-update) | async-done | bytes 9437200 | tf_op jit(solution)/shard_map/all_gather | solution.py:69
  249.8 7.5 convolution_convert_fusion.3
  257.3 112.0 %all-gather.4.cloned.1.call-done = bf16[16,384,768]{2,1,0:T(8,128)(2,1)} async-done(((bf16[16,192,768]{2,1,0:T(8,128)(2,1)}), bf16[16,384,768]{2,1,0:T(8,128)(2,1)}) %all-gather.4.cloned.1.call-update) | async-done | bytes 9437200 | tf_op jit(solution)/shard_map/all_gather | solution.py:71
  369.3 7.4 fusion.14
  377.6 4.3 scatter_custom_fusion
  382.2 10.0 %all_to_all.20 = bf16[4,2,136]{2,1,0:T(2,128)(2,1)S(1)} all-to-all(bf16[4,2,136]{2,1,0:T(2,128)(2,1)S(1)} %reshape.339), channel_id=1, replica_groups=mesh['groups'=2,'expert'=4,'dp'=2,'inner'=2] {'expert'}, dimensions={0} | all-to-all | bytes 4352 | tf_op jit(solution)/shard_map/all_to_all | solution.py:66
  392.4 7.0 all-reduce.3.cloned.1.call-done
  399.4 8.3 %convolution_convert_fusion.2 = bf16[16,768,384]{1,2,0:T(8,128)(2,1)} fusion(bf16[16,68,768]{2,0,1:T(8,128)(2,1)S(1)} %bitcast.61, bf16[16,68,384]{2,1,0:T(8,128)(2,1)} %get-tuple-element.21, bf16[16,68,384]{2,1,0:T(8,128)(2,1)} %get-tuple-element.20, bf16[16,68,384]{2,1,0:T(8,128)(2,1)} %get-tuple-element.22, f32[16,68]{1,0:T(8,128)S(1)} %reshape.263), kind=kOutput, calls=%fused_computation.10 | convolution fusion | flops 652296192 | bytes 13619456 | tf_op jit(solution)/shard_map/jrd,jrf->jdf/dot_general | solution.py:131
  407.9 8.2 %convolution_convert_fusion.1 = bf16[16,768,384]{1,2,0:T(8,128)(2,1)} fusion(bf16[16,68,768]{2,0,1:T(8,128)(2,1)S(1)} %bitcast.62, bf16[16,68,384]{2,1,0:T(8,128)(2,1)} %get-tuple-element.20, f32[16,68]{1,0:T(8,128)S(1)} %reshape.263, bf16[16,68,384]{2,1,0:T(8,128)(2,1)} %get-tuple-element.22), kind=kOutput, calls=%fused_computation.9 | convolution fusion | flops 650207232 | bytes 12783872 | tf_op jit(solution)/shard_map/jrd,jrf->jdf/dot_general | solution.py:134
  417.3 7.7 %convolution_convert_fusion = bf16[16,384,768]{2,1,0:T(8,128)(2,1)} fusion(bf16[16,68,768]{2,0,1:T(8,128)(2,1)S(1)} %multiply_convert_fusion, bf16[16,68,384]{2,1,0:T(8,128)(2,1)S(1)} %copy-done.4, bf16[16,68,384]{2,1,0:T(8,128)(2,1)} %get-tuple-element.22), kind=kOutput, calls=%fused_computation.8 | convolution fusion | flops 649789440 | bytes 12779520 | tf_op jit(solution)/shard_map/jrf,jrd->jfd/dot_general | solution.py:136
  425.1 1.1 copy-done.3
  426.2 6.0 fusion.43
  432.2 0.7 slice-done.2
  433.1 2.0 add_convert_fusion
  435.4 1.2 dynamic-slice_bitcast_fusion.3
  436.6 3.6 collective-permute-start.2
  440.1 1.1 collective-permute-start
  441.2 0.8 fusion.2
  442.2 0.7 reshape.341
  442.9 4.2 all-to-all-start.3
  447.1 29.7 %all-to-all-done.3 = bf16[4,2,136]{2,1,0:T(2,128)(2,1)S(1)} async-done(((bf16[4,2,136]{2,1,0:T(2,128)(2,1)}), bf16[4,2,136]{2,1,0:T(2,128)(2,1)S(1)}, u32[]{:S(2)}, u32[]{:S(2)}) %all-to-all-start.3) | async-done | bytes 2208 | tf_op jit(solution)/shard_map/all_to_all | solution.py:118
  477.0 6.8 gather_fusion.4
  484.6 0.8 copy-done.6
  485.3 1.3 maximum_bitcast_fusion
  487.3 2.2 copy.62
  489.5 2.7 reshape_reshape.7
  492.2 4.0 gather_fusion.3
  496.2 1.7 bitcast_reduce_fusion
  497.9 21.6 %reduce-scatter.4.cloned.1.call-done = bf16[16,768,192]{1,2,0:T(8,128)(2,1)} async-done(((bf16[16,768,384]{1,2,0:T(8,128)(2,1)}), bf16[16,768,192]{1,2,0:T(8,128)(2,1)}) %reduce-scatter.4.cloned.1.call-update) | async-done | bytes 4718608 | tf_op jit(solution)/shard_map/reduce_scatter | solution.py:138
  519.5 113.3 %reduce-scatter.6.cloned.1.call-done = bf16[16,768,192]{1,2,0:T(8,128)(2,1)} async-done(((bf16[16,768,384]{1,2,0:T(8,128)(2,1)}), bf16[16,768,192]{1,2,0:T(8,128)(2,1)}) %reduce-scatter.6.cloned.1.call-update) | async-done | bytes 4718608 | tf_op jit(solution)/shard_map/reduce_scatter | solution.py:141
  632.9 113.5 %reduce-scatter.8.cloned.1.call-done = bf16[16,192,768]{2,1,0:T(8,128)(2,1)} async-done(((bf16[16,384,768]{2,1,0:T(8,128)(2,1)}), bf16[16,192,768]{2,1,0:T(8,128)(2,1)}) %reduce-scatter.8.cloned.1.call-update) | async-done | bytes 4718608 | tf_op jit(solution)/shard_map/reduce_scatter | solution.py:144
  (80 shorter events, 7.5 us)
Async XLA Ops:
  7.2 25.7 %copy-start = (bf16[128,768]{1,0:T(8,128)(2,1)S(1)}, bf16[128,768]{1,0:T(8,128)(2,1)}, u32[]{:S(2)}) copy-start(bf16[128,768]{1,0:T(8,128)(2,1)} %param.7) | copy-start | bytes 589828
  7.2 123.1 %all-gather.6.cloned.1.call-start = ((), (), s32[]{:S(2)}) async-start(), calls=%async_computation.8 | async-start | bytes 14155776 | tf_op jit(solution)/shard_map/all_gather | solution.py:70
  7.9 241.9 %all-gather.8.cloned.1.call-start = ((), (), s32[]{:S(2)}) async-start(), calls=%async_computation.9 | async-start | bytes 14155776 | tf_op jit(solution)/shard_map/all_gather | solution.py:69
  8.7 0.7 copy-start.7
  8.7 360.6 %all-gather.4.cloned.1.call-start = ((), (), s32[]{:S(2)}) async-start(), calls=%async_computation.7 | async-start | bytes 14155776 | tf_op jit(solution)/shard_map/all_gather | solution.py:71
  37.7 10.3 %copy-start.2 = (bf16[128,768]{1,0:T(8,128)(2,1)S(1)}, bf16[128,768]{1,0:T(8,128)(2,1)}, u32[]{:S(2)}) copy-start(bf16[128,768]{1,0:T(8,128)(2,1)} %param.8) | copy-start | bytes 589828
  61.9 45.4 %all-to-all-start.2 = ((bf16[16,4,17,768]{3,0,2,1:T(8,128)(2,1)}), bf16[16,4,17,768]{3,0,2,1:T(8,128)(2,1)S(1)}, u32[]{:S(2)}, u32[]{:S(2)}) async-start(bf16[16,4,17,768]{3,0,2,1:T(8,128)(2,1)} %copy.58), calls=%async_computation.2 | async-start | bytes 3342336 | tf_op jit(solution)/shard_map/all_to_all | solution.py:64
  107.3 150.0 %all-to-all-start.1 = ((bf16[16,4,17,768]{3,0,2,1:T(8,128)(2,1)}), bf16[16,4,17,768]{3,0,2,1:T(8,128)(2,1)S(1)}, u32[]{:S(2)}, u32[]{:S(2)}) async-start(bf16[16,4,17,768]{3,0,2,1:T(8,128)(2,1)} %copy.56), calls=%async_computation.1 | async-start | bytes 3342336 | tf_op jit(solution)/shard_map/all_to_all | solution.py:65
  110.9 288.5 %all-reduce.3.cloned.1.call-start = ((), (), s32[]{:S(2)}) async-start(), calls=%async_computation.13 | async-start | bytes 5308416 | tf_op jit(solution)/shard_map/psum | solution.py:90
  376.8 0.7 copy-start.8
  376.8 142.8 %reduce-scatter.4.cloned.1.call-start = ((), (), s32[]{:S(2)}) async-start(), calls=%async_computation.10 | async-start | bytes 14155776 | tf_op jit(solution)/shard_map/reduce_scatter | solution.py:138
  407.7 225.2 %reduce-scatter.6.cloned.1.call-start = ((), (), s32[]{:S(2)}) async-start(), calls=%async_computation.11 | async-start | bytes 14155776 | tf_op jit(solution)/shard_map/reduce_scatter | solution.py:141
  416.1 1.2 copy-start.4
  416.2 330.2 %reduce-scatter.8.cloned.1.call-start = ((), (), s32[]{:S(2)}) async-start(), calls=%async_computation.12 | async-start | bytes 14155776 | tf_op jit(solution)/shard_map/reduce_scatter | solution.py:144
  425.0 1.2 copy-start.3
  425.0 7.2 slice-start
  426.2 6.0 slice-start.1
  426.2 6.7 slice-start.2
  426.2 6.9 copy-start.5
  436.6 48.0 %collective-permute-start.2 = (bf16[16,1,17,768]{3,0,2,1:T(8,128)(2,1)}, bf16[16,1,17,768]{3,0,2,1:T(8,128)(2,1)S(1)}, u32[]{:S(2)}, u32[]{:S(2)}) collective-permute-start(bf16[16,1,17,768]{3,0,2,1:T(8,128)(2,1)} %get-tuple-element.24), channel_id=1, source_target_pairs={{0,12},{4,0},{8,4},{12,8},{1,13},{5,1},{9,5},{13,9},{2,14},{6,2},{... | collective-permute-start | bytes 1253384 | tf_op jit(solution)/shard_map/ppermute | solution.py:110
  440.1 44.4 %collective-permute-start.1 = (bf16[16,1,17,768]{3,0,2,1:T(8,128)(2,1)}, bf16[16,1,17,768]{3,0,2,1:T(8,128)(2,1)S(1)}, u32[]{:S(2)}, u32[]{:S(2)}) collective-permute-start(bf16[16,1,17,768]{3,0,2,1:T(8,128)(2,1)} %get-tuple-element.25), channel_id=1, source_target_pairs={{0,8},{4,12},{8,0},{12,4},{1,9},{5,13},{9,1},{13,5},{2,10},{6,14},... | collective-permute-start | bytes 1253384 | tf_op jit(solution)/shard_map/ppermute | solution.py:110
  440.1 44.4 %collective-permute-start = (bf16[16,1,17,768]{3,0,2,1:T(8,128)(2,1)}, bf16[16,1,17,768]{3,0,2,1:T(8,128)(2,1)}, u32[]{:S(2)}, u32[]{:S(2)}) collective-permute-start(bf16[16,1,17,768]{3,0,2,1:T(8,128)(2,1)} %get-tuple-element.26), channel_id=1, source_target_pairs={{0,4},{4,8},{8,12},{12,0},{1,5},{5,9},{9,13},{13,1},{2,6},{6,10},{... | collective-permute-start | bytes 1253384 | tf_op jit(solution)/shard_map/ppermute | solution.py:110
  442.9 33.9 %all-to-all-start.3 = ((bf16[4,2,136]{2,1,0:T(2,128)(2,1)}), bf16[4,2,136]{2,1,0:T(2,128)(2,1)S(1)}, u32[]{:S(2)}, u32[]{:S(2)}) async-start(bf16[4,2,136]{2,1,0:T(2,128)(2,1)} %reshape.341), calls=%async_computation.3 | async-start | bytes 8192 | tf_op jit(solution)/shard_map/all_to_all | solution.py:118
  484.6 0.8 copy-start.6
  492.2 254.1 %copy-start.1 = (bf16[128,768]{1,0:T(8,128)(2,1)S(1)}, bf16[128,768]{1,0:T(8,128)(2,1)}, u32[]{:S(2)}) copy-start(bf16[128,768]{1,0:T(8,128)(2,1)} %param.7) | copy-start | bytes 589828
Sparse Core Ops, SparseCore 0:
  9.6 120.6 all-gather.5
  131.8 117.9 all-gather.7
  251.4 117.8 all-gather.3
  376.9 22.4 all-reduce.2
  407.8 111.6 reduce-scatter.3
  522.3 110.5 reduce-scatter.5
  635.8 110.5 reduce-scatter.7
